TPU v7x, 32 devices: a whole 2x2x4 slice. The times are simulated.
32 devices in a mesh: section: 4 (over y, x), expert: 8 (over z, core).
Axes of the slice: x: 2, y: 2, z: 4, core: 2. Of those that a mesh axis runs over, the one named last changes fastest.
Arguments:
- sent_fwd: bfloat16 [4, 512, 3584], P('section', 'expert'), may hold values from -6 to 6
- sent_bwd: bfloat16 [4, 512, 3584], P('section', 'expert'), may hold values from -6 to 6
- router_w: float32 [4, 3584, 4], P('section'), may hold values from -0.5 to 0.5
- w_up: bfloat16 [4, 3584, 4096], P('section', None, 'expert'), may hold values from -0.09375 to 0.09375
- w_down: bfloat16 [4, 4096, 3584], P('section', 'expert'), may hold values from -0.1875 to 0.1875
- routes_fwd: int32 [4, 512, 1], P('section', 'expert'), may hold values from 0 to 3; in each aligned block of 64 rows (0 to 63, 64 to 127, ..., all dimensions but the last counted through in order) at most 17 rows name the same one
- routes_bwd: int32 [4, 512, 1], P('section', 'expert'), may hold values from 0 to 3; in each aligned block of 64 rows (0 to 63, 64 to 127, ..., all dimensions but the last counted through in order) at most 17 rows name the same one
Outputs:
- out_fwd: bfloat16 [4, 512, 3584], P('section', 'expert')
- out_bwd: bfloat16 [4, 512, 3584], P('section', 'expert')
Inputs may be any that keep to these rules, and one draw needn't show every extreme that they name: `routes_fwd`: at each section the 64 rows of one device name any one expert at most 17 times in all, a bound that some block reaches. `routes_bwd`: at each section the 64 rows of one device name any one expert at most 17 times in all, a bound that some block reaches.
All inputs are finite; a program needn't handle non-finite values.
Results may differ from a plain program's by a relative error of at most 0.003.
Values may be sent and summed in bfloat16 or wider, within the bound.
A program may use at most 128 MiB of HBM per device.

v0:
```python
import jax
import jax.numpy as jnp
from jax import lax
from jax.sharding import PartitionSpec as P

EXPERTS = 4
CAP = 17


def from_behind(block, axis, distance):
    devices = range(lax.axis_size(axis))
    route = [((i - distance) % len(devices), i) for i in devices]
    return lax.ppermute(block, axis, route)


def prepare(inputs, routes, slices):
    tokens_here = inputs.shape[0]
    model_width = inputs.shape[1]
    chosen = routes.reshape(-1)
    onehot = (chosen[:, None] == jnp.arange(EXPERTS, dtype=jnp.int32)[None, :]).astype(jnp.int32)
    position = jnp.sum((jnp.cumsum(onehot, axis=0) - 1) * onehot, axis=1)
    slot_index = chosen * CAP + position
    per_token = slot_index.reshape(tokens_here, -1)
    targets = jnp.arange(EXPERTS * CAP, dtype=jnp.int32)
    placing = jnp.sum(
        (per_token[None, :, :] == targets[:, None, None]).astype(jnp.float32), axis=2
    ).astype(jnp.bfloat16)
    packed = jnp.dot(placing, inputs, preferred_element_type=jnp.float32).astype(jnp.bfloat16)
    outbox = jnp.broadcast_to(
        packed.reshape(EXPERTS, 1, CAP, model_width), (EXPERTS, slices, CAP, model_width)
    )
    outbox = outbox.reshape(EXPERTS * slices, CAP, model_width)
    picking = onehot.reshape(tokens_here, -1, EXPERTS).astype(jnp.float32)
    return (outbox, slot_index, picking)


def finish(inputs, returned, slot_index, picking, router, slices):
    tokens_here = inputs.shape[0]
    model_width = inputs.shape[1]
    summed = jnp.sum(
        returned.astype(jnp.float32).reshape(EXPERTS, slices, CAP, model_width), axis=1
    )
    summed = summed.reshape(EXPERTS * CAP, model_width)
    gathered = jnp.take(summed, slot_index, axis=0).reshape(tokens_here, -1, model_width)
    logits = jnp.dot(inputs.astype(jnp.float32), router, precision=lax.Precision.HIGHEST)
    picked = jnp.sum(logits[:, None, :] * picking, axis=2)
    scores = jax.nn.sigmoid(picked)
    mixed = inputs.astype(jnp.float32) + jnp.sum(scores[:, :, None] * gathered, axis=1)
    return mixed.astype(jnp.bfloat16)[None]


def on_device(sent_fwd, sent_bwd, router_w, w_up, w_down, routes_fwd, routes_bwd):
    inputs_fwd = from_behind(sent_fwd, "section", 1)[0]
    inputs_bwd = from_behind(sent_bwd, "section", -1)[0]
    slices = lax.axis_size("expert") // EXPERTS
    router = router_w[0]
    up_local = w_up[0]
    down_local = w_down[0]
    outbox_fwd, slots_fwd, picking_fwd = prepare(inputs_fwd, routes_fwd[0], slices)
    outbox_bwd, slots_bwd, picking_bwd = prepare(inputs_bwd, routes_bwd[0], slices)
    outbox = jnp.concatenate((outbox_fwd, outbox_bwd), axis=1)
    received = lax.all_to_all(outbox, "expert", split_axis=0, concat_axis=0, tiled=True)
    sources = received.shape[0]
    slot_count = received.shape[1]
    rows_in = received.reshape(sources * slot_count, received.shape[2])
    hidden = jax.nn.silu(jnp.dot(rows_in, up_local, preferred_element_type=jnp.float32)).astype(
        jnp.bfloat16
    )
    partial_out = jnp.dot(hidden, down_local, preferred_element_type=jnp.float32).astype(
        jnp.bfloat16
    )
    computed = partial_out.reshape(sources, slot_count, partial_out.shape[1])
    returned = lax.all_to_all(computed, "expert", split_axis=0, concat_axis=0, tiled=True)
    returned_fwd = returned[:, :CAP]
    returned_bwd = returned[:, CAP:]
    out_fwd = finish(inputs_fwd, returned_fwd, slots_fwd, picking_fwd, router, slices)
    out_bwd = finish(inputs_bwd, returned_bwd, slots_bwd, picking_bwd, router, slices)
    return (out_fwd, out_bwd)


def solution(mesh):
    return jax.shard_map(
        on_device,
        mesh=mesh,
        in_specs=(
            P("section", "expert", None),
            P("section", "expert", None),
            P("section", None, None),
            P("section", None, "expert"),
            P("section", "expert", None),
            P("section", "expert", None),
            P("section", "expert", None),
        ),
        out_specs=(P("section", "expert", None), P("section", "expert", None)),
        check_vma=False,
    )
```

profile of v0, /device:TPU:1, one launch (start us, length us, event | category | flops | bytes accessed | tf_op | source)
XLA Modules:
  0.0 160.1 jit_solution(10059187049002012492)
XLA Ops:
  0.6 0.0 copy-start
  0.6 3.0 %collective-permute-start.1 = (bf16[1,64,3584]{2,1,0:T(8,128)(2,1)}, bf16[1,64,3584]{2,1,0:T(8,128)(2,1)S(1)}, u32[]{:S(2)}, u32[]{:S(2)}) collective-permute-start(bf16[1,64,3584]{2,1,0:T(8,128)(2,1)} %param.10), channel_id=1, source_target_pairs={{8,0},{16,8},{24,16},{0,24},{9,1},{17,9},{25,17},{1,25},{10,2},{18... | collective-permute-start | bytes 1376264 | tf_op jit(solution)/shard_map/ppermute | solution.py:13
  3.7 0.0 collective-permute-start
  3.7 0.7 fusion.24
  4.3 0.1 copy.15
  4.4 0.1 reduce_window_sum.18
  4.5 0.1 copy.16
  4.6 0.7 select_reduce_fusion
  5.3 0.7 fusion.25
  6.0 0.1 copy.13
  6.1 0.1 reduce_window_sum.17
  6.1 0.1 copy.14
  6.2 0.7 select_reduce_fusion.1
  6.9 0.7 fusion.26
  7.6 0.7 fusion.27
  8.2 5.0 %collective-permute-done.1 = bf16[1,64,3584]{2,1,0:T(8,128)(2,1)S(1)} collective-permute-done((bf16[1,64,3584]{2,1,0:T(8,128)(2,1)}, bf16[1,64,3584]{2,1,0:T(8,128)(2,1)S(1)}, u32[]{:S(2)}, u32[]{:S(2)}) %collective-permute-start.1) | collective-permute-done | bytes 458784 | tf_op jit(solution)/shard_map/ppermute | solution.py:13
  13.2 0.0 copy-start.2
  13.2 0.4 convolution_convert_fusion.1
  13.6 0.2 broadcast_in_dim.19
  13.8 10.2 %collective-permute-done = bf16[1,64,3584]{2,1,0:T(8,128)(2,1)S(1)} collective-permute-done((bf16[1,64,3584]{2,1,0:T(8,128)(2,1)}, bf16[1,64,3584]{2,1,0:T(8,128)(2,1)S(1)}, u32[]{:S(2)}, u32[]{:S(2)}) %collective-permute-start) | collective-permute-done | bytes 458784 | tf_op jit(solution)/shard_map/ppermute | solution.py:13
  23.9 0.0 copy-start.4
  23.9 0.4 convolution_convert_fusion.2
  24.3 0.2 broadcast_in_dim.17
  24.5 0.1 broadcast_in_dim.20
  24.6 0.1 broadcast_in_dim.18
  24.7 0.4 pad_maximum_fusion
  25.1 58.5 %all_to_all.10 = bf16[8,34,3584]{2,1,0:T(8,128)(2,1)S(1)} all-to-all(bf16[8,34,3584]{2,1,0:T(8,128)(2,1)S(1)} %pad_maximum_fusion), channel_id=1, replica_groups=mesh['section'=4,'expert'=8] {'expert'}, dimensions={0} | all-to-all | bytes 3899392 | tf_op jit(solution)/shard_map/all_to_all | solution.py:62
  83.6 1.6 reshape.219
  85.2 6.0 %convolution_convert_fusion = bf16[272,3584]{1,0:T(8,128)(2,1)S(1)} fusion(bf16[1,512,3584]{2,1,0:T(8,128)(2,1)} %param.13, bf16[272,3584]{1,0:T(8,128)(2,1)} %reshape.219, bf16[1,3584,512]{2,1,0:T(8,128)(2,1)} %param.12), kind=kOutput, calls=%fused_computation.2 | convolution fusion | flops 1998159872 | bytes 11239424 | tf_op jit(solution)/shard_map/dot_general | solution.py:69
  91.2 1.7 %reshape.220 = bf16[8,34,3584]{2,1,0:T(8,128)(2,1)} reshape(bf16[272,3584]{1,0:T(8,128)(2,1)S(1)} %convolution_convert_fusion) | data formatting | bytes 3899392 | tf_op jit(solution)/shard_map/reshape | solution.py:72
  92.9 0.0 copy-start.8
  92.9 0.0 copy-start.7
  92.9 4.6 %all-to-all-start.1 = ((bf16[8,34,3584]{2,1,0:T(8,128)(2,1)}), bf16[8,34,3584]{2,1,0:T(8,128)(2,1)S(1)}, u32[]{:S(2)}, u32[]{:S(2)}) async-start(bf16[8,34,3584]{2,1,0:T(8,128)(2,1)} %reshape.220), calls=%async_computation.1 | async-start | bytes 4587520 | tf_op jit(solution)/shard_map/all_to_all | solution.py:73
  97.5 0.0 copy-done.8
  97.6 0.0 copy-done.7
  97.6 0.0 copy-done.2
  97.6 0.0 copy-done
  97.6 0.5 fusion.4
  98.1 0.0 copy-done.4
  98.1 0.5 fusion.3
  98.6 51.2 %all-to-all-done.1 = bf16[8,34,3584]{2,1,0:T(8,128)(2,1)S(1)} async-done(((bf16[8,34,3584]{2,1,0:T(8,128)(2,1)}), bf16[8,34,3584]{2,1,0:T(8,128)(2,1)S(1)}, u32[]{:S(2)}, u32[]{:S(2)}) %all-to-all-start.1) | async-done | bytes 1949728 | tf_op jit(solution)/shard_map/all_to_all | solution.py:73
  149.9 2.2 %convert_reduce_fusion = (f32[4,17,3584]{2,1,0:T(8,128)}, f32[4,17,3584]{2,1,0:T(8,128)}) fusion(bf16[8,34,3584]{2,1,0:T(8,128)(2,1)S(1)} %all-to-all-done.1), kind=kLoop, calls=%fused_computation.8 | loop fusion | flops 1462272 | bytes 3899392 | tf_op jit(solution)/shard_map/reduce_sum | solution.py:40
  152.0 0.0 copy-start.1
  152.0 1.6 reshape.223
  153.6 0.2 copy-done.1
  153.8 0.2 reshape.226
  154.0 1.8 %gather_fusion = f32[64,3584]{1,0:T(8,128)} fusion(f32[68,3584]{1,0:T(8,128)S(1)} %reshape.223, s32[1024]{0:T(1024)S(1)} %pad_clamp_fusion.1), kind=kCustom, calls=%fused_computation.clone | custom fusion | bytes 1835264 | tf_op jit(solution)/shard_map/jit(_take)/gather | solution.py:44
  155.8 0.0 copy-start.3
  155.8 0.0 copy-start.5
  155.8 0.0 copy-start.6
  155.8 1.8 %gather_fusion.1 = f32[64,3584]{1,0:T(8,128)} fusion(f32[68,3584]{1,0:T(8,128)S(1)} %reshape.226, s32[1024]{0:T(1024)S(1)} %pad_clamp_fusion), kind=kCustom, calls=%fused_computation.1.clone | custom fusion | bytes 1835264 | tf_op jit(solution)/shard_map/jit(_take)/gather | solution.py:44
  157.6 0.0 copy-done.3
  157.6 0.0 copy-done.5
  157.6 0.0 copy-done.6
  157.6 2.5 %fusion.5 = (bf16[1,64,3584]{2,1,0:T(8,128)(2,1)}, bf16[1,64,3584]{2,1,0:T(8,128)(2,1)}) fusion(f32[64,3584]{1,0:T(8,128)} %gather_fusion.1, bf16[1,64,3584]{2,1,0:T(8,128)(2,1)S(1)} %copy-done.3, f32[64]{0:T(128)S(1)} %add_divide_fusion, pred[64]{0:T(512)(128)(4,1)S(1)} %get-tuple-element.5, f32[64,3584]{1,0:T(8,128)S(1)} %copy-done.6, ...), kind=kLoop, calls=%fused_computation.16 | loop fusion | flops 2293760 | bytes 3670656 | tf_op jit(solution)/shard_map/convert_element_type | solution.py:49
  (6 shorter events, 0.0 us)
Async XLA Ops:
  0.6 97.0 %copy-start = (f32[1,3584,4]{1,2,0:T(4,128)S(1)}, f32[1,3584,4]{1,2,0:T(4,128)}, u32[]{:S(2)}) copy-start(f32[1,3584,4]{1,2,0:T(4,128)} %param.11) | copy-start | bytes 172036
  0.6 12.6 %collective-permute-start.1 = (bf16[1,64,3584]{2,1,0:T(8,128)(2,1)}, bf16[1,64,3584]{2,1,0:T(8,128)(2,1)S(1)}, u32[]{:S(2)}, u32[]{:S(2)}) collective-permute-start(bf16[1,64,3584]{2,1,0:T(8,128)(2,1)} %param.10), channel_id=1, source_target_pairs={{8,0},{16,8},{24,16},{0,24},{9,1},{17,9},{25,17},{1,25},{10,2},{18... | collective-permute-start | bytes 1376264 | tf_op jit(solution)/shard_map/ppermute | solution.py:13
  3.7 20.2 %collective-permute-start = (bf16[1,64,3584]{2,1,0:T(8,128)(2,1)}, bf16[1,64,3584]{2,1,0:T(8,128)(2,1)S(1)}, u32[]{:S(2)}, u32[]{:S(2)}) collective-permute-start(bf16[1,64,3584]{2,1,0:T(8,128)(2,1)} %param.9), channel_id=1, source_target_pairs={{24,0},{0,8},{8,16},{16,24},{25,1},{1,9},{9,17},{17,25},{26,2},{2,... | collective-permute-start | bytes 1376264 | tf_op jit(solution)/shard_map/ppermute | solution.py:13
  13.2 84.4 %copy-start.2 = (bf16[1,64,3584]{2,1,0:T(8,128)(2,1)}, bf16[1,64,3584]{2,1,0:T(8,128)(2,1)S(1)}, u32[]{:S(2)}) copy-start(bf16[1,64,3584]{2,1,0:T(8,128)(2,1)S(1)} %collective-permute-done.1) | copy-start | bytes 1376260
  23.9 74.2 %copy-start.4 = (bf16[1,64,3584]{2,1,0:T(8,128)(2,1)}, bf16[1,64,3584]{2,1,0:T(8,128)(2,1)S(1)}, u32[]{:S(2)}) copy-start(bf16[1,64,3584]{2,1,0:T(8,128)(2,1)S(1)} %collective-permute-done) | copy-start | bytes 1376260
  92.9 4.6 %copy-start.8 = (s32[1,64,1]{1,2,0:T(1,128)S(1)}, s32[1,64,1]{1,2,0:T(1,128)}, u32[]{:S(2)}) copy-start(s32[1,64,1]{1,2,0:T(1,128)} %param.14) | copy-start | bytes 772
  92.9 4.6 %copy-start.7 = (s32[1,64,1]{1,2,0:T(1,128)S(1)}, s32[1,64,1]{1,2,0:T(1,128)}, u32[]{:S(2)}) copy-start(s32[1,64,1]{1,2,0:T(1,128)} %param.15) | copy-start | bytes 772
  92.9 56.9 %all-to-all-start.1 = ((bf16[8,34,3584]{2,1,0:T(8,128)(2,1)}), bf16[8,34,3584]{2,1,0:T(8,128)(2,1)S(1)}, u32[]{:S(2)}, u32[]{:S(2)}) async-start(bf16[8,34,3584]{2,1,0:T(8,128)(2,1)} %reshape.220), calls=%async_computation.1 | async-start | bytes 4587520 | tf_op jit(solution)/shard_map/all_to_all | solution.py:73
  152.0 1.8 %copy-start.1 = (f32[4,17,3584]{2,1,0:T(8,128)S(1)}, f32[4,17,3584]{2,1,0:T(8,128)}, u32[]{:S(2)}) copy-start(f32[4,17,3584]{2,1,0:T(8,128)} %get-tuple-element.3) | copy-start | bytes 2924548
  155.8 1.8 %copy-start.3 = (bf16[1,64,3584]{2,1,0:T(8,128)(2,1)S(1)}, bf16[1,64,3584]{2,1,0:T(8,128)(2,1)}, u32[]{:S(2)}) copy-start(bf16[1,64,3584]{2,1,0:T(8,128)(2,1)} %copy-done.2) | copy-start | bytes 1376260
  155.8 1.8 %copy-start.5 = (bf16[1,64,3584]{2,1,0:T(8,128)(2,1)S(1)}, bf16[1,64,3584]{2,1,0:T(8,128)(2,1)}, u32[]{:S(2)}) copy-start(bf16[1,64,3584]{2,1,0:T(8,128)(2,1)} %copy-done.4) | copy-start | bytes 1376260
  155.8 1.8 %copy-start.6 = (f32[64,3584]{1,0:T(8,128)S(1)}, f32[64,3584]{1,0:T(8,128)}, u32[]{:S(2)}) copy-start(f32[64,3584]{1,0:T(8,128)} %gather_fusion) | copy-start | bytes 2752516
where the time goes:
time: 161 us; the launch traced here: 160 us
  waiting for transfers between devices  66.4 us (41%)
  blocking collectives  58.5 us (36%)
  local copies, waits for them, and re-layouts  9.66 us (6%)
  other arithmetic  9.4 us (6%)
  matrix products  7.74 us (5%)
  starting transfers between devices  7.64 us (5%)
    all_to_all x1, blocking collectives, on_device(): lax.all_to_all(outbox, 'expert', split_axis=0, concat_axis=0, tiled=True)  58.5 us
    all_to_all x1, waiting for transfers between devices, on_device(): lax.all_to_all(computed, 'expert', split_axis=0, concat_axis=0, tiled=True)  51.2 us
    ppermute x2, waiting for transfers between devices, from_behind(): return lax.ppermute(block, axis, route)  15.1 us
    dot_general x1, matrix products, on_device(): jnp.dot(hidden, down_local, preferred_element_type=jnp.float32)  6.05 us
    all_to_all x1, starting transfers between devices, on_device(): lax.all_to_all(computed, 'expert', split_axis=0, concat_axis=0, tiled=True)  4.6 us
    gather x2, local copies, waits for them, and re-layouts, finish(): jnp.take(summed, slot_index, axis=0).reshape(tokens_here, -1, model_width)  3.61 us
  transfers between devices with their start and end apart: 3, of which 3 were waited for; matrix products, arithmetic and copies ran while one was open for 4% of the time, Pallas kernels for 0%

commit v1 on v0

v1 whole, which is shorter than its diff:
```python
import functools

import jax
import jax.numpy as jnp
from jax import lax
from jax.experimental import pallas as pl
from jax.experimental.pallas import tpu as pltpu
from jax.sharding import PartitionSpec as P

EXPERTS = 4
CAP = 17
PIECES = 2
MESH = pl.DeviceIdType.MESH
F32 = jnp.float32
BF16 = jnp.bfloat16
NT = (((1,), (1,)), ((), ()))


def layer_kernel(
    dims,
    rt_ref, fwd_ref, bwd_ref, router_ref, up_hbm, down_hbm,
    out_fwd, out_bwd,
    x_buf, pack_buf, mine, theirs, acc, hid, part_out, part_in, own_part, y_out, y_in,
    out_buf, up_ref, down_ref, place, place_t, rt_sib, logit_out, logit_in, score_ref,
    relay_s, relay_r, disp_s, disp_r, pair_s, pair_r, part_s, part_r, ret_s, ret_r,
    fin_s, fin_r, loc_s, w_sem, small_s, small_r,
):
    chips, per_expert, sections, tokens, rows, padded, pieces, width = dims
    half = pieces * width
    both = 2 * tokens
    section = lax.axis_index("section")
    me = lax.axis_index("expert")
    core = lax.rem(me, 2)
    chip = me // 2
    sib = {"section": section, "expert": chip * 2 + 1 - core}
    after = lax.rem(section + 1, sections)
    before = lax.rem(section + sections - 1, sections)

    def at_chip(distance):
        return {
            "section": section,
            "expert": lax.rem(chip + distance + chips, chips) * 2 + core,
        }

    def remote(src, dst, send, recv, device):
        return pltpu.make_async_remote_copy(
            src_ref=src, dst_ref=dst, send_sem=send, recv_sem=recv,
            device_id=device, device_id_type=MESH,
        )

    def arrived(dst, send, recv):
        remote(dst, dst, send, recv, sib).wait_recv()

    w_up_copy = pltpu.make_async_copy(up_hbm, up_ref, w_sem.at[0])
    w_down_copy = pltpu.make_async_copy(down_hbm, down_ref, w_sem.at[1])

    tail = padded - 16
    zeros = jnp.zeros((pieces, chips, 16, width), BF16)
    mine[:, :, tail:padded, :] = zeros
    theirs[:, :, tail:padded, :] = zeros
    y_in[:, :, tail:padded, :] = zeros

    barrier = pltpu.get_barrier_semaphore()
    greet = [sib]
    for there in (after, before):
        for j in range(2):
            greet.append({"section": there, "expert": chip * 2 + j})
    for d in range(1, chips):
        greet.append(at_chip(d))
    for device in greet:
        pl.semaphore_signal(barrier, inc=1, device_id=device, device_id_type=MESH)
    pl.semaphore_wait(barrier, len(greet))

    sends = []
    small = remote(rt_ref, rt_sib, small_s.at[0], small_r.at[0], sib)
    small.start()
    sends.append(small)
    for k in range(pieces):
        for m, (source, there) in enumerate(((fwd_ref, after), (bwd_ref, before))):
            for j in range(2):
                copy = remote(
                    source.at[:, pl.ds(j * half + k * width, width)],
                    x_buf.at[k, pl.ds(pl.multiple_of(core * both + m * tokens, tokens), tokens), :],
                    relay_s.at[k, j, m], relay_r.at[k, core, m],
                    {"section": there, "expert": chip * 2 + j},
                )
                copy.start()
                sends.append(copy)
    w_up_copy.start()
    w_down_copy.start()

    small.wait_recv()
    own_routes, sib_routes = rt_ref[...], rt_sib[...]
    first = core == 0
    chosen = jnp.concatenate(
        (jnp.where(first, own_routes, sib_routes), jnp.where(first, sib_routes, own_routes)),
        axis=1,
    )
    count = 2 * both
    named = lax.broadcasted_iota(jnp.int32, (8, count), 0) == chosen
    onehot = jnp.where(named, 1.0, 0.0).astype(F32)
    earlier = lax.broadcasted_iota(jnp.int32, (count, count), 0) <= lax.broadcasted_iota(
        jnp.int32, (count, count), 1
    )
    tri = jnp.where(earlier, 1.0, 0.0).astype(BF16)
    counted = jnp.dot(onehot.astype(BF16), tri, preferred_element_type=F32)
    position = jnp.sum(onehot * (counted - 1.0), axis=0, keepdims=True)
    slots = lax.broadcasted_iota(jnp.int32, (padded, count), 0).astype(F32)
    for d in range(chips):
        expert = lax.rem(chip + d, chips) // per_expert
        here = jnp.where(chosen[0:1, :] == expert, position, -1.0)
        place[d * padded:(d + 1) * padded, :] = jnp.where(slots == here, 1.0, 0.0).astype(BF16)
    eye = lax.broadcasted_iota(jnp.int32, (count, count), 0) == lax.broadcasted_iota(
        jnp.int32, (count, count), 1
    )
    eye = jnp.where(eye, 1.0, 0.0).astype(BF16)
    place_t[...] = lax.dot_general(eye, place[...], NT, preferred_element_type=F32).astype(BF16)

    mine_cols = core * half
    their_cols = (1 - core) * half

    def pair(k, d):
        copy = remote(mine.at[k, d], theirs.at[k, d], pair_s.at[k, d], pair_r.at[k, d], sib)
        copy.start()
        sends.append(copy)

    def stage_pack(k):
        for j in range(2):
            for m in range(2):
                arrived(
                    x_buf.at[k, pl.ds(j * both + m * tokens, tokens), :],
                    relay_s.at[k, j, m], relay_r.at[k, j, m],
                )
        packed = jnp.dot(place[...], x_buf[k], preferred_element_type=F32).astype(BF16)
        packed = packed.reshape(chips, padded, width)
        pack_buf[k] = packed[1:]
        mine[k, 0] = packed[0]
        for d in range(1, chips):
            copy = remote(
                pack_buf.at[k, d - 1, pl.ds(0, rows), :], mine.at[k, d, pl.ds(0, rows), :],
                disp_s.at[k, d], disp_r.at[k, d], at_chip(d),
            )
            copy.start()
            sends.append(copy)
        pair(k, 0)
        cols = pl.ds(pl.multiple_of(mine_cols + k * width, 128), width)
        term = lax.dot_general(
            router_ref[:, cols], x_buf[k].astype(F32), NT,
            precision=lax.Precision.HIGHEST, preferred_element_type=F32,
        )
        logit_out[...] = term if k == 0 else logit_out[...] + term

    def stage_forward(k):
        for d in range(1, chips):
            arrived(mine.at[k, d, pl.ds(0, rows), :], disp_s.at[k, d], disp_r.at[k, d])
            pair(k, d)

    def stage_up(k):
        for d in range(chips):
            arrived(theirs.at[k, d], pair_s.at[k, d], pair_r.at[k, d])
        if k == 0:
            w_up_copy.wait()
        total = jnp.dot(
            mine[k].reshape(chips * padded, width),
            up_ref[pl.ds(pl.multiple_of(mine_cols + k * width, 128), width), :],
            preferred_element_type=F32,
        )
        total += jnp.dot(
            theirs[k].reshape(chips * padded, width),
            up_ref[pl.ds(pl.multiple_of(their_cols + k * width, 128), width), :],
            preferred_element_type=F32,
        )
        acc[...] = total if k == 0 else acc[...] + total

    for step in range(pieces + 2):
        if step < pieces:
            stage_pack(step)
        if step == pieces:
            logits = remote(logit_out, logit_in, small_s.at[1], small_r.at[1], sib)
            logits.start()
            sends.append(logits)
        if 0 <= step - 1 < pieces:
            stage_forward(step - 1)
        if 0 <= step - 2:
            stage_up(step - 2)

    hid[...] = jax.nn.silu(acc[...]).astype(BF16)
    w_down_copy.wait()

    def stage_down(k):
        other = jnp.dot(
            hid[...], down_ref[:, pl.ds(pl.multiple_of(their_cols + k * width, 128), width)],
            preferred_element_type=F32,
        )
        part_out[k] = other.astype(BF16)
        copy = remote(part_out.at[k], part_in.at[k], part_s.at[k], part_r.at[k], sib)
        copy.start()
        sends.append(copy)
        own_part[k] = jnp.dot(
            hid[...], down_ref[:, pl.ds(pl.multiple_of(mine_cols + k * width, 128), width)],
            preferred_element_type=F32,
        ).astype(BF16)

    def stage_return(k):
        arrived(part_in.at[k], part_s.at[k], part_r.at[k])
        y = (own_part[k].astype(F32) + part_in[k].astype(F32)).astype(BF16)
        y = y.reshape(chips, padded, width)
        y_out[k] = y[1:]
        y_in[k, 0, 0:rows, :] = y[0, 0:rows]
        for d in range(1, chips):
            copy = remote(
                y_out.at[k, d - 1, pl.ds(0, rows), :], y_in.at[k, d, pl.ds(0, rows), :],
                ret_s.at[k, d], ret_r.at[k, d], at_chip(-d),
            )
            copy.start()
            sends.append(copy)

    for step in range(pieces + 1):
        if step < pieces:
            stage_down(step)
        if 0 <= step - 1:
            stage_return(step - 1)

    logits.wait_recv()
    picked = jnp.sum(onehot * (logit_out[...] + logit_in[...]), axis=0, keepdims=True)
    score = jax.nn.sigmoid(picked)
    score_ref[...] = jnp.transpose(jnp.broadcast_to(score, (128, count)))

    locals_ = []
    for k in range(pieces):
        for d in range(1, chips):
            arrived(y_in.at[k, d, pl.ds(0, rows), :], ret_s.at[k, d], ret_r.at[k, d])
        gathered = jnp.dot(
            place_t[...], y_in[k].reshape(chips * padded, width), preferred_element_type=F32
        )
        mixed = x_buf[k].astype(F32) + score_ref[:, 0:1] * gathered
        out_buf[k] = mixed.astype(BF16)
        cols = pl.ds(pl.multiple_of(mine_cols + k * width, 128), width)
        for m, out in enumerate((out_fwd, out_bwd)):
            theirs_at = pl.multiple_of((1 - core) * both + m * tokens, tokens)
            copy = remote(
                out_buf.at[k, pl.ds(theirs_at, tokens), :], out.at[:, cols],
                fin_s.at[k, m], fin_r.at[k, m], sib,
            )
            copy.start()
            sends.append(copy)
            mine_at = pl.multiple_of(core * both + m * tokens, tokens)
            local = pltpu.make_async_copy(
                out_buf.at[k, pl.ds(mine_at, tokens), :], out.at[:, cols], loc_s.at[k, m]
            )
            local.start()
            locals_.append(local)

    for local in locals_:
        local.wait()
    for k in range(pieces):
        other_cols = pl.ds(pl.multiple_of(their_cols + k * width, 128), width)
        for m, out in enumerate((out_fwd, out_bwd)):
            arrived(out.at[:, other_cols], fin_s.at[k, m], fin_r.at[k, m])
    for copy in sends:
        copy.wait_send()


def on_device(sent_fwd, sent_bwd, router_w, w_up, w_down, routes_fwd, routes_bwd):
    tokens, model_width = sent_fwd.shape[1:]
    hidden = w_up.shape[2]
    sections = lax.axis_size("section")
    chips = lax.axis_size("expert") // 2
    per_expert = chips // EXPERTS
    rows = -(-4 * CAP // 8) * 8
    padded = -(-4 * CAP // 16) * 16
    pieces = PIECES
    width = model_width // 2 // pieces
    count = 4 * tokens
    dims = (chips, per_expert, sections, tokens, rows, padded, pieces, width)
    routes = jnp.concatenate((routes_fwd.reshape(1, tokens), routes_bwd.reshape(1, tokens)), axis=1)
    routes = jnp.broadcast_to(routes, (8, 2 * tokens))
    router = jnp.pad(router_w[0].T, ((0, 8 - EXPERTS), (0, 0)))
    total = chips * padded
    dma = pltpu.SemaphoreType.DMA
    any_space = pl.BlockSpec(memory_space=pl.ANY)
    vmem = pl.BlockSpec(memory_space=pltpu.VMEM)
    shape = jax.ShapeDtypeStruct((tokens, model_width), BF16)
    out_fwd, out_bwd = pl.pallas_call(
        functools.partial(layer_kernel, dims),
        out_shape=(shape, shape),
        in_specs=[vmem, any_space, any_space, vmem, any_space, any_space],
        out_specs=(any_space, any_space),
        scratch_shapes=[
            pltpu.VMEM((pieces, count, width), BF16),
            pltpu.VMEM((pieces, chips - 1, padded, width), BF16),
            pltpu.VMEM((pieces, chips, padded, width), BF16),
            pltpu.VMEM((pieces, chips, padded, width), BF16),
            pltpu.VMEM((total, hidden), F32),
            pltpu.VMEM((total, hidden), BF16),
            pltpu.VMEM((pieces, total, width), BF16),
            pltpu.VMEM((pieces, total, width), BF16),
            pltpu.VMEM((pieces, total, width), BF16),
            pltpu.VMEM((pieces, chips - 1, padded, width), BF16),
            pltpu.VMEM((pieces, chips, padded, width), BF16),
            pltpu.VMEM((pieces, count, width), BF16),
            pltpu.VMEM((model_width, hidden), BF16),
            pltpu.VMEM((hidden, model_width), BF16),
            pltpu.VMEM((total, count), BF16),
            pltpu.VMEM((count, total), BF16),
            pltpu.VMEM((8, 2 * tokens), jnp.int32),
            pltpu.VMEM((8, count), F32),
            pltpu.VMEM((8, count), F32),
            pltpu.VMEM((count, 128), F32),
            dma((pieces, 2, 2)), dma((pieces, 2, 2)),
            dma((pieces, chips)), dma((pieces, chips)),
            dma((pieces, chips)), dma((pieces, chips)),
            dma((pieces,)), dma((pieces,)),
            dma((pieces, chips)), dma((pieces, chips)),
            dma((pieces, 2)), dma((pieces, 2)),
            dma((pieces, 2)), dma((2,)), dma((2,)), dma((2,)),
        ],
        compiler_params=pltpu.CompilerParams(collective_id=0, has_side_effects=True),
    )(routes, sent_fwd[0], sent_bwd[0], router, w_up[0], w_down[0])
    return out_fwd[None], out_bwd[None]


def solution(mesh):
    return jax.shard_map(
        on_device,
        mesh=mesh,
        in_specs=(
            P("section", "expert", None),
            P("section", "expert", None),
            P("section", None, None),
            P("section", None, "expert"),
            P("section", "expert", None),
            P("section", "expert", None),
            P("section", "expert", None),
        ),
        out_specs=(P("section", "expert", None), P("section", "expert", None)),
        check_vma=False,
    )
```

time: 161 us -> 79.3 us (0.49)
  Pallas kernels: 0 us -> 71.8 us
  waiting for transfers between devices: 66.4 us -> 0 us
  blocking collectives: 58.5 us -> 0 us
  other arithmetic: 9.4 us -> 0.75 us
  matrix products: 7.74 us -> 0 us
  starting transfers between devices: 7.64 us -> 0 us
  local copies, waits for them, and re-layouts: 9.66 us -> 5.7 us
    pallas_call x0 -> x1, Pallas kernels: none -> 71.8 us  [on_device(): pl.pallas_call(functools.partial(layer_kernel, dims), out_shape=(shape, s...]
    all_to_all x1 -> x0, blocking collectives: 58.5 us -> none  [on_device(): lax.all_to_all(outbox, 'expert', split_axis=0, concat_axis=0, tiled=True)]
    all_to_all x1 -> x0, waiting for transfers between devices: 51.2 us -> none  [on_device(): lax.all_to_all(computed, 'expert', split_axis=0, concat_axis=0, tiled=True)]
    ppermute x2 -> x0, waiting for transfers between devices: 15.1 us -> none  [from_behind(): return lax.ppermute(block, axis, route)]
    dot_general x5 -> x0, matrix products: 7.74 us -> none  [the longest x1 6.05 us: on_device(): jnp.dot(hidden, down_local, preferred_element_type=jnp.float32)]
    reshape x4 -> x0, local copies, waits for them, and re-layouts: 5.01 us -> none  [the longest x2 1.75 us: finish(): summed = summed.reshape(EXPERTS * CAP, model_width)]
    all_to_all x1 -> x0, starting transfers between devices: 4.6 us -> none  [on_device(): lax.all_to_all(computed, 'expert', split_axis=0, concat_axis=0, tiled=True)]
    convert_element_type x3 -> x0, other arithmetic: 3.85 us -> none  [the longest x1 2.54 us: finish(): return mixed.astype(jnp.bfloat16)[None]]
  transfers between devices with their start and end apart: 3 -> 0, of which waited for: 3 -> 0; matrix products, arithmetic and copies ran while one was open for 4% -> 0% of each run, Pallas kernels for 0% -> 0%
where the time goes in v1:
time: 79.3 us; the launch traced here: 78.9 us
  Pallas kernels  71.8 us (91%)
  local copies, waits for them, and re-layouts  5.7 us (7%)
    pallas_call x1, Pallas kernels, on_device(): pl.pallas_call(functools.partial(layer_kernel, dims), out_shape=(shape, s...  71.8 us
    unnamed x2, local copies, waits for them, and re-layouts  3.63 us

profile of v1, /device:TPU:1, one launch (start us, length us, event | category | flops | bytes accessed | tf_op | source)
XLA Modules:
  0.0 78.9 jit_solution(17591175264675192600)
XLA Ops:
  0.6 0.7 add_bitcast_fusion
  1.4 0.6 broadcast_in_dim.14.rt_ref
  2.0 1.5 %pad.4.router_ref = f32[8,3584]{1,0:T(8,128)} pad(f32[4,3584]{1,0:T(4,128)} %bitcast.19, f32[]{:T(128)} %constant.2.clone.1), padding=0_4x0_0 | pad | bytes 172036 | tf_op jit(solution)/shard_map/jit(_pad)/pad | solution.py:278
  3.4 71.8 %shard_map.86 = (bf16[64,3584]{1,0:T(8,128)(2,1)}, bf16[64,3584]{1,0:T(8,128)(2,1)}) custom-call(s32[8,128]{1,0:T(8,128)} %broadcast_in_dim.14.rt_ref, bf16[64,3584]{1,0:T(8,128)(2,1)} %bitcast.17, bf16[64,3584]{1,0:T(8,128)(2,1)} %bitcast.18, f32[8,3584]{1,0:T(8,128)} %pad.4.router_ref, bf16[3584,512]{1,0:T(8,128)(2,1)} %bitcast.13, bf16[512,3584]{1,0:T(8,128)(2,1)} %bitcast.14), custom_call_target="tpu_custom_call" | custom-call | tf_op jit(solution)/shard_map/pallas_call | solution.py:284
  75.3 1.8 %copy.11 = bf16[1,64,3584]{2,1,0:T(8,128)(2,1)} copy(bf16[1,64,3584]{2,1,0:T(8,128)(2,1)} %bitcast.16) | data formatting | bytes 917504
  77.1 1.8 %copy.12 = bf16[1,64,3584]{2,1,0:T(8,128)(2,1)} copy(bf16[1,64,3584]{2,1,0:T(8,128)(2,1)} %bitcast.15) | data formatting | bytes 917504

commit v2 on v1

--- a/solution.py
+++ b/solution.py
@@ -9,7 +9,7 @@
 
 EXPERTS = 4
 CAP = 17
-PIECES = 2
+PIECES = 7
 MESH = pl.DeviceIdType.MESH
 F32 = jnp.float32
 BF16 = jnp.bfloat16

time: 79.3 us -> 75 us (0.946)
  Pallas kernels: 71.8 us -> 66.8 us
    pallas_call x1, Pallas kernels: 71.8 us -> 66.8 us  [on_device(): pl.pallas_call(functools.partial(layer_kernel, dims), out_shape=(shape, s...]
where the time goes in v2:
time: 75 us; the launch traced here: 73.9 us
  Pallas kernels  66.8 us (89%)
  local copies, waits for them, and re-layouts  5.7 us (8%)
  other arithmetic  0.75 us (1%)
    pallas_call x1, Pallas kernels, on_device(): pl.pallas_call(functools.partial(layer_kernel, dims), out_shape=(shape, s...  66.8 us
    unnamed x2, local copies, waits for them, and re-layouts  3.63 us

profile of v2, /device:TPU:1, one launch (start us, length us, event | category | flops | bytes accessed | tf_op | source)
XLA Modules:
  0.0 73.9 jit_solution(12487741750437614545)
XLA Ops:
  0.6 0.7 %add_bitcast_fusion = s32[128]{0:T(128)S(1)} fusion(s32[1,64]{1,0:T(1,128)} %bitcast.20, s32[1,64]{1,0:T(1,128)} %bitcast.21), kind=kLoop, calls=%fused_computation | loop fusion | flops 128 | bytes 1024 | tf_op jit(solution)/shard_map/broadcast_in_dim | solution.py:277
  1.4 0.6 broadcast_in_dim.14.rt_ref
  2.0 1.5 %pad.4.router_ref = f32[8,3584]{1,0:T(8,128)} pad(f32[4,3584]{1,0:T(4,128)} %bitcast.19, f32[]{:T(128)} %constant.2.clone.1), padding=0_4x0_0 | pad | bytes 172036 | tf_op jit(solution)/shard_map/jit(_pad)/pad | solution.py:278
  3.4 66.8 %shard_map.86 = (bf16[64,3584]{1,0:T(8,128)(2,1)}, bf16[64,3584]{1,0:T(8,128)(2,1)}) custom-call(s32[8,128]{1,0:T(8,128)} %broadcast_in_dim.14.rt_ref, bf16[64,3584]{1,0:T(8,128)(2,1)} %bitcast.17, bf16[64,3584]{1,0:T(8,128)(2,1)} %bitcast.18, f32[8,3584]{1,0:T(8,128)} %pad.4.router_ref, bf16[3584,512]{1,0:T(8,128)(2,1)} %bitcast.13, bf16[512,3584]{1,0:T(8,128)(2,1)} %bitcast.14), custom_call_target="tpu_custom_call" | custom-call | tf_op jit(solution)/shard_map/pallas_call | solution.py:284
  70.2 1.8 %copy.11 = bf16[1,64,3584]{2,1,0:T(8,128)(2,1)} copy(bf16[1,64,3584]{2,1,0:T(8,128)(2,1)} %bitcast.16) | data formatting | bytes 917504
  72.0 1.8 %copy.12 = bf16[1,64,3584]{2,1,0:T(8,128)(2,1)} copy(bf16[1,64,3584]{2,1,0:T(8,128)(2,1)} %bitcast.15) | data formatting | bytes 917504

commit v3 on v2

--- a/solution.py
+++ b/solution.py
@@ -18,7 +18,7 @@
 
 def layer_kernel(
     dims,
-    rt_ref, fwd_ref, bwd_ref, router_ref, up_hbm, down_hbm,
+    rf_ref, rb_ref, fwd_ref, bwd_ref, router_ref, up_hbm, down_hbm,
     out_fwd, out_bwd,
     x_buf, pack_buf, mine, theirs, acc, hid, part_out, part_in, own_part, y_out, y_in,
     out_buf, up_ref, down_ref, place, place_t, rt_sib, logit_out, logit_in, score_ref,
@@ -36,11 +36,18 @@
     after = lax.rem(section + 1, sections)
     before = lax.rem(section + sections - 1, sections)
 
-    def at_chip(distance):
-        return {
-            "section": section,
-            "expert": lax.rem(chip + distance + chips, chips) * 2 + core,
-        }
+    def partner(v):
+        other, bit = chip, 1
+        while bit <= v:
+            if (v // bit) % 2:
+                other = other + bit - 2 * bit * lax.rem(chip // bit, 2)
+            bit *= 2
+        return other
+
+    def at_chip(v):
+        return {"section": section, "expert": partner(v) * 2 + core}
+
+    order = [v for v in range(chips // 2, chips)] + [v for v in range(1, chips // 2)]
 
     def remote(src, dst, send, recv, device):
         return pltpu.make_async_remote_copy(
@@ -65,16 +72,19 @@
     for there in (after, before):
         for j in range(2):
             greet.append({"section": there, "expert": chip * 2 + j})
-    for d in range(1, chips):
+    for d in order:
         greet.append(at_chip(d))
     for device in greet:
         pl.semaphore_signal(barrier, inc=1, device_id=device, device_id_type=MESH)
     pl.semaphore_wait(barrier, len(greet))
 
     sends = []
-    small = remote(rt_ref, rt_sib, small_s.at[0], small_r.at[0], sib)
-    small.start()
-    sends.append(small)
+    route_copies = []
+    for m, ref in enumerate((rf_ref, rb_ref)):
+        copy = remote(ref, rt_sib.at[m], small_s.at[m], small_r.at[m], sib)
+        copy.start()
+        sends.append(copy)
+        route_copies.append(copy)
     for k in range(pieces):
         for m, (source, there) in enumerate(((fwd_ref, after), (bwd_ref, before))):
             for j in range(2):
@@ -89,15 +99,18 @@
     w_up_copy.start()
     w_down_copy.start()
 
-    small.wait_recv()
-    own_routes, sib_routes = rt_ref[...], rt_sib[...]
+    for copy in route_copies:
+        copy.wait_recv()
+    own = (rf_ref[...], rb_ref[...])
+    sibs = (rt_sib[0], rt_sib[1])
     first = core == 0
     chosen = jnp.concatenate(
-        (jnp.where(first, own_routes, sib_routes), jnp.where(first, sib_routes, own_routes)),
+        [jnp.where(first, a, b) for a, b in zip(own, sibs)]
+        + [jnp.where(first, b, a) for a, b in zip(own, sibs)],
         axis=1,
     )
     count = 2 * both
-    named = lax.broadcasted_iota(jnp.int32, (8, count), 0) == chosen
+    named = lax.broadcasted_iota(jnp.int32, (EXPERTS, count), 0) == chosen
     onehot = jnp.where(named, 1.0, 0.0).astype(F32)
     earlier = lax.broadcasted_iota(jnp.int32, (count, count), 0) <= lax.broadcasted_iota(
         jnp.int32, (count, count), 1
@@ -107,8 +120,8 @@
     position = jnp.sum(onehot * (counted - 1.0), axis=0, keepdims=True)
     slots = lax.broadcasted_iota(jnp.int32, (padded, count), 0).astype(F32)
     for d in range(chips):
-        expert = lax.rem(chip + d, chips) // per_expert
-        here = jnp.where(chosen[0:1, :] == expert, position, -1.0)
+        expert = partner(d) // per_expert
+        here = jnp.where(chosen == expert, position, -1.0)
         place[d * padded:(d + 1) * padded, :] = jnp.where(slots == here, 1.0, 0.0).astype(BF16)
     eye = lax.broadcasted_iota(jnp.int32, (count, count), 0) == lax.broadcasted_iota(
         jnp.int32, (count, count), 1
@@ -135,7 +148,7 @@
         packed = packed.reshape(chips, padded, width)
         pack_buf[k] = packed[1:]
         mine[k, 0] = packed[0]
-        for d in range(1, chips):
+        for d in order:
             copy = remote(
                 pack_buf.at[k, d - 1, pl.ds(0, rows), :], mine.at[k, d, pl.ds(0, rows), :],
                 disp_s.at[k, d], disp_r.at[k, d], at_chip(d),
@@ -151,7 +164,7 @@
         logit_out[...] = term if k == 0 else logit_out[...] + term
 
     def stage_forward(k):
-        for d in range(1, chips):
+        for d in order:
             arrived(mine.at[k, d, pl.ds(0, rows), :], disp_s.at[k, d], disp_r.at[k, d])
             pair(k, d)
 
@@ -176,7 +189,7 @@
         if step < pieces:
             stage_pack(step)
         if step == pieces:
-            logits = remote(logit_out, logit_in, small_s.at[1], small_r.at[1], sib)
+            logits = remote(logit_out, logit_in, small_s.at[2], small_r.at[2], sib)
             logits.start()
             sends.append(logits)
         if 0 <= step - 1 < pieces:
@@ -207,10 +220,10 @@
         y = y.reshape(chips, padded, width)
         y_out[k] = y[1:]
         y_in[k, 0, 0:rows, :] = y[0, 0:rows]
-        for d in range(1, chips):
+        for d in order:
             copy = remote(
                 y_out.at[k, d - 1, pl.ds(0, rows), :], y_in.at[k, d, pl.ds(0, rows), :],
-                ret_s.at[k, d], ret_r.at[k, d], at_chip(-d),
+                ret_s.at[k, d], ret_r.at[k, d], at_chip(d),
             )
             copy.start()
             sends.append(copy)
@@ -261,6 +274,19 @@
         copy.wait_send()
 
 
+def write_kernel(a_ref, b_ref, out_a, out_b, held, in_sem, out_sem):
+    pairs = ((a_ref, out_a), (b_ref, out_b))
+    loads = [pltpu.make_async_copy(src, held.at[i], in_sem.at[i]) for i, (src, _) in enumerate(pairs)]
+    stores = [pltpu.make_async_copy(held.at[i], dst, out_sem.at[i]) for i, (_, dst) in enumerate(pairs)]
+    for load in loads:
+        load.start()
+    for load, store in zip(loads, stores):
+        load.wait()
+        store.start()
+    for store in stores:
+        store.wait()
+
+
 def on_device(sent_fwd, sent_bwd, router_w, w_up, w_down, routes_fwd, routes_bwd):
     tokens, model_width = sent_fwd.shape[1:]
     hidden = w_up.shape[2]
@@ -273,9 +299,7 @@
     width = model_width // 2 // pieces
     count = 4 * tokens
     dims = (chips, per_expert, sections, tokens, rows, padded, pieces, width)
-    routes = jnp.concatenate((routes_fwd.reshape(1, tokens), routes_bwd.reshape(1, tokens)), axis=1)
-    routes = jnp.broadcast_to(routes, (8, 2 * tokens))
-    router = jnp.pad(router_w[0].T, ((0, 8 - EXPERTS), (0, 0)))
+    router = router_w[0].T
     total = chips * padded
     dma = pltpu.SemaphoreType.DMA
     any_space = pl.BlockSpec(memory_space=pl.ANY)
@@ -284,7 +308,7 @@
     out_fwd, out_bwd = pl.pallas_call(
         functools.partial(layer_kernel, dims),
         out_shape=(shape, shape),
-        in_specs=[vmem, any_space, any_space, vmem, any_space, any_space],
+        in_specs=[vmem, vmem, any_space, any_space, vmem, any_space, any_space],
         out_specs=(any_space, any_space),
         scratch_shapes=[
             pltpu.VMEM((pieces, count, width), BF16),
@@ -303,9 +327,9 @@
             pltpu.VMEM((hidden, model_width), BF16),
             pltpu.VMEM((total, count), BF16),
             pltpu.VMEM((count, total), BF16),
-            pltpu.VMEM((8, 2 * tokens), jnp.int32),
-            pltpu.VMEM((8, count), F32),
-            pltpu.VMEM((8, count), F32),
+            pltpu.VMEM((2, 1, tokens), jnp.int32),
+            pltpu.VMEM((EXPERTS, count), F32),
+            pltpu.VMEM((EXPERTS, count), F32),
             pltpu.VMEM((count, 128), F32),
             dma((pieces, 2, 2)), dma((pieces, 2, 2)),
             dma((pieces, chips)), dma((pieces, chips)),
@@ -313,10 +337,21 @@
             dma((pieces,)), dma((pieces,)),
             dma((pieces, chips)), dma((pieces, chips)),
             dma((pieces, 2)), dma((pieces, 2)),
-            dma((pieces, 2)), dma((2,)), dma((2,)), dma((2,)),
+            dma((pieces, 2)), dma((2,)), dma((3,)), dma((3,)),
         ],
         compiler_params=pltpu.CompilerParams(collective_id=0, has_side_effects=True),
-    )(routes, sent_fwd[0], sent_bwd[0], router, w_up[0], w_down[0])
+    )(
+        routes_fwd.reshape(1, tokens), routes_bwd.reshape(1, tokens),
+        sent_fwd[0], sent_bwd[0], router, w_up[0], w_down[0],
+    )
+    out_fwd, out_bwd = pl.pallas_call(
+        write_kernel,
+        out_shape=(shape, shape),
+        in_specs=[any_space, any_space],
+        out_specs=(any_space, any_space),
+        scratch_shapes=[pltpu.VMEM((2, tokens, model_width), BF16), dma((2,)), dma((2,))],
+        compiler_params=pltpu.CompilerParams(has_side_effects=True),
+    )(out_fwd, out_bwd)
     return out_fwd[None], out_bwd[None]
 
 

time: 75 us -> 69.6 us (0.928); the launches traced: 73.9 us -> 69.4 us
  local copies, waits for them, and re-layouts: 5.7 us -> 0 us
  Pallas kernels: 66.8 us -> 68.7 us
  other arithmetic: 0.75 us -> 0 us
    unnamed x2 -> x0, local copies, waits for them, and re-layouts: 3.63 us -> none
    pallas_call x0 -> x1, Pallas kernels: none -> 1.97 us  [on_device(): pl.pallas_call(write_kernel, out_shape=(shape, shape), in_specs=[any_spac...]
    pad x1 -> x0, local copies, waits for them, and re-layouts: 1.47 us -> none  [on_device(): router = jnp.pad(router_w[0].T, ((0, 8 - EXPERTS), (0, 0)))]
where the time goes in v3:
time: 69.6 us; the launch traced here: 69.4 us
  Pallas kernels  68.7 us (99%)
    pallas_call x1, Pallas kernels, on_device(): pl.pallas_call(functools.partial(layer_kernel, dims), out_shape=(shape, s...  66.8 us
    pallas_call x1, Pallas kernels, on_device(): pl.pallas_call(write_kernel, out_shape=(shape, shape), in_specs=[any_spac...  1.97 us

profile of v3, /device:TPU:1, one launch (start us, length us, event | category | flops | bytes accessed | tf_op | source)
XLA Modules:
  0.0 69.4 jit_solution(119549755918331981)
XLA Ops:
  0.6 66.8 %shard_map.86 = (bf16[64,3584]{1,0:T(8,128)(2,1)}, bf16[64,3584]{1,0:T(8,128)(2,1)}) custom-call(s32[1,64]{1,0:T(1,128)} %bitcast.16, s32[1,64]{1,0:T(1,128)} %bitcast.17, bf16[64,3584]{1,0:T(8,128)(2,1)} %bitcast.13, bf16[64,3584]{1,0:T(8,128)(2,1)} %bitcast.14, f32[4,3584]{1,0:T(4,128)} %bitcast.15, bf16[3584,512]{1,0:T(8,128)(2,1)} %bitcast.11, ...), custom_call_target="tpu_custom_call" | custom-call | tf_op jit(solution)/shard_map/pallas_call | solution.py:308
  67.4 2.0 %shard_map.87 = (bf16[64,3584]{1,0:T(8,128)(2,1)}, bf16[64,3584]{1,0:T(8,128)(2,1)}) custom-call(bf16[64,3584]{1,0:T(8,128)(2,1)} %get-tuple-element.6.a_ref, bf16[64,3584]{1,0:T(8,128)(2,1)} %get-tuple-element.7.b_ref), custom_call_target="tpu_custom_call" | custom-call | tf_op jit(solution)/shard_map/pallas_call | solution.py:347

commit v4 on v3

--- a/solution.py
+++ b/solution.py
@@ -9,7 +9,7 @@
 
 EXPERTS = 4
 CAP = 17
-PIECES = 7
+PIECES = 14
 MESH = pl.DeviceIdType.MESH
 F32 = jnp.float32
 BF16 = jnp.bfloat16

time: 69.6 us -> 79.5 us (1.14)
  Pallas kernels: 68.7 us -> 78.6 us
    pallas_call x1, Pallas kernels: 66.8 us -> 76.7 us  [on_device(): pl.pallas_call(functools.partial(layer_kernel, dims), out_shape=(shape, s...]
where the time goes in v4:
time: 79.5 us; the launch traced here: 79.3 us
  Pallas kernels  78.6 us (99%)
    pallas_call x1, Pallas kernels, on_device(): pl.pallas_call(functools.partial(layer_kernel, dims), out_shape=(shape, s...  76.7 us
    pallas_call x1, Pallas kernels, on_device(): pl.pallas_call(write_kernel, out_shape=(shape, shape), in_specs=[any_spac...  1.97 us

profile of v4, /device:TPU:1, one launch (start us, length us, event | category | flops | bytes accessed | tf_op | source)
XLA Modules:
  0.0 79.3 jit_solution(237914653541092346)
XLA Ops:
  0.6 76.7 %shard_map.86 = (bf16[64,3584]{1,0:T(8,128)(2,1)}, bf16[64,3584]{1,0:T(8,128)(2,1)}) custom-call(s32[1,64]{1,0:T(1,128)} %bitcast.16, s32[1,64]{1,0:T(1,128)} %bitcast.17, bf16[64,3584]{1,0:T(8,128)(2,1)} %bitcast.13, bf16[64,3584]{1,0:T(8,128)(2,1)} %bitcast.14, f32[4,3584]{1,0:T(4,128)} %bitcast.15, bf16[3584,512]{1,0:T(8,128)(2,1)} %bitcast.11, ...), custom_call_target="tpu_custom_call" | custom-call | tf_op jit(solution)/shard_map/pallas_call | solution.py:308
  77.3 2.0 %shard_map.87 = (bf16[64,3584]{1,0:T(8,128)(2,1)}, bf16[64,3584]{1,0:T(8,128)(2,1)}) custom-call(bf16[64,3584]{1,0:T(8,128)(2,1)} %get-tuple-element.6.a_ref, bf16[64,3584]{1,0:T(8,128)(2,1)} %get-tuple-element.7.b_ref), custom_call_target="tpu_custom_call" | custom-call | tf_op jit(solution)/shard_map/pallas_call | solution.py:347

commit v5 on v3

--- a/solution.py
+++ b/solution.py
@@ -156,12 +156,6 @@
             copy.start()
             sends.append(copy)
         pair(k, 0)
-        cols = pl.ds(pl.multiple_of(mine_cols + k * width, 128), width)
-        term = lax.dot_general(
-            router_ref[:, cols], x_buf[k].astype(F32), NT,
-            precision=lax.Precision.HIGHEST, preferred_element_type=F32,
-        )
-        logit_out[...] = term if k == 0 else logit_out[...] + term
 
     def stage_forward(k):
         for d in order:
@@ -169,8 +163,6 @@
             pair(k, d)
 
     def stage_up(k):
-        for d in range(chips):
-            arrived(theirs.at[k, d], pair_s.at[k, d], pair_r.at[k, d])
         if k == 0:
             w_up_copy.wait()
         total = jnp.dot(
@@ -178,6 +170,8 @@
             up_ref[pl.ds(pl.multiple_of(mine_cols + k * width, 128), width), :],
             preferred_element_type=F32,
         )
+        for d in range(chips):
+            arrived(theirs.at[k, d], pair_s.at[k, d], pair_r.at[k, d])
         total += jnp.dot(
             theirs[k].reshape(chips * padded, width),
             up_ref[pl.ds(pl.multiple_of(their_cols + k * width, 128), width), :],
@@ -188,13 +182,11 @@
     for step in range(pieces + 2):
         if step < pieces:
             stage_pack(step)
-        if step == pieces:
-            logits = remote(logit_out, logit_in, small_s.at[2], small_r.at[2], sib)
-            logits.start()
-            sends.append(logits)
+        if step >= pieces:
+            stage_up(step - 2)
         if 0 <= step - 1 < pieces:
             stage_forward(step - 1)
-        if 0 <= step - 2:
+        if 0 <= step - 2 < pieces - 2:
             stage_up(step - 2)
 
     hid[...] = jax.nn.silu(acc[...]).astype(BF16)
@@ -234,6 +226,16 @@
         if 0 <= step - 1:
             stage_return(step - 1)
 
+    for k in range(pieces):
+        cols = pl.ds(pl.multiple_of(mine_cols + k * width, 128), width)
+        term = lax.dot_general(
+            router_ref[:, cols], x_buf[k].astype(F32), NT,
+            precision=lax.Precision.HIGHEST, preferred_element_type=F32,
+        )
+        logit_out[...] = term if k == 0 else logit_out[...] + term
+    logits = remote(logit_out, logit_in, small_s.at[2], small_r.at[2], sib)
+    logits.start()
+    sends.append(logits)
     logits.wait_recv()
     picked = jnp.sum(onehot * (logit_out[...] + logit_in[...]), axis=0, keepdims=True)
     score = jax.nn.sigmoid(picked)

time: 69.6 us -> 69.4 us (level)
  no operation moved by 1% of the time
where the time goes in v5:
time: 69.4 us; the launch traced here: 69.2 us
  Pallas kernels  68.6 us (99%)
    pallas_call x1, Pallas kernels, on_device(): pl.pallas_call(functools.partial(layer_kernel, dims), out_shape=(shape, s...  66.6 us
    pallas_call x1, Pallas kernels, on_device(): pl.pallas_call(write_kernel, out_shape=(shape, shape), in_specs=[any_spac...  1.97 us

profile of v5, /device:TPU:1, one launch (start us, length us, event | category | flops | bytes accessed | tf_op | source)
XLA Modules:
  0.0 69.2 jit_solution(18277283980656594415)
XLA Ops:
  0.6 66.6 %shard_map.86 = (bf16[64,3584]{1,0:T(8,128)(2,1)}, bf16[64,3584]{1,0:T(8,128)(2,1)}) custom-call(s32[1,64]{1,0:T(1,128)} %bitcast.16, s32[1,64]{1,0:T(1,128)} %bitcast.17, bf16[64,3584]{1,0:T(8,128)(2,1)} %bitcast.13, bf16[64,3584]{1,0:T(8,128)(2,1)} %bitcast.14, f32[4,3584]{1,0:T(4,128)} %bitcast.15, bf16[3584,512]{1,0:T(8,128)(2,1)} %bitcast.11, ...), custom_call_target="tpu_custom_call" | custom-call | tf_op jit(solution)/shard_map/pallas_call | solution.py:310
  67.2 2.0 %shard_map.87 = (bf16[64,3584]{1,0:T(8,128)(2,1)}, bf16[64,3584]{1,0:T(8,128)(2,1)}) custom-call(bf16[64,3584]{1,0:T(8,128)(2,1)} %get-tuple-element.6.a_ref, bf16[64,3584]{1,0:T(8,128)(2,1)} %get-tuple-element.7.b_ref), custom_call_target="tpu_custom_call" | custom-call | tf_op jit(solution)/shard_map/pallas_call | solution.py:349

commit v6 on v5

--- a/solution.py
+++ b/solution.py
@@ -18,9 +18,9 @@
 
 def layer_kernel(
     dims,
-    rf_ref, rb_ref, fwd_ref, bwd_ref, router_ref, up_hbm, down_hbm,
+    rf_ref, rb_ref, fwd_hbm, bwd_hbm, router_ref, up_hbm, down_hbm,
     out_fwd, out_bwd,
-    x_buf, pack_buf, mine, theirs, acc, hid, part_out, part_in, own_part, y_out, y_in,
+    fwd_ref, bwd_ref, in_s, x_buf, pack_buf, mine, theirs, acc, hid, part_out, part_in, own_part, y_out, y_in,
     out_buf, up_ref, down_ref, place, place_t, rt_sib, logit_out, logit_in, score_ref,
     relay_s, relay_r, disp_s, disp_r, pair_s, pair_r, part_s, part_r, ret_s, ret_r,
     fin_s, fin_r, loc_s, w_sem, small_s, small_r,
@@ -61,6 +61,13 @@
     w_up_copy = pltpu.make_async_copy(up_hbm, up_ref, w_sem.at[0])
     w_down_copy = pltpu.make_async_copy(down_hbm, down_ref, w_sem.at[1])
 
+    loads = [
+        pltpu.make_async_copy(fwd_hbm, fwd_ref, in_s.at[0]),
+        pltpu.make_async_copy(bwd_hbm, bwd_ref, in_s.at[1]),
+    ]
+    for load in loads:
+        load.start()
+
     tail = padded - 16
     zeros = jnp.zeros((pieces, chips, 16, width), BF16)
     mine[:, :, tail:padded, :] = zeros
@@ -77,6 +84,8 @@
     for device in greet:
         pl.semaphore_signal(barrier, inc=1, device_id=device, device_id_type=MESH)
     pl.semaphore_wait(barrier, len(greet))
+    for load in loads:
+        load.wait()
 
     sends = []
     route_copies = []
@@ -313,6 +322,9 @@
         in_specs=[vmem, vmem, any_space, any_space, vmem, any_space, any_space],
         out_specs=(any_space, any_space),
         scratch_shapes=[
+            pltpu.VMEM((tokens, model_width), BF16),
+            pltpu.VMEM((tokens, model_width), BF16),
+            dma((2,)),
             pltpu.VMEM((pieces, count, width), BF16),
             pltpu.VMEM((pieces, chips - 1, padded, width), BF16),
             pltpu.VMEM((pieces, chips, padded, width), BF16),

time: 69.4 us -> 69.2 us (level)
  no operation moved by 1% of the time
where the time goes in v6:
time: 69.2 us; the launch traced here: 69 us
  Pallas kernels  68.4 us (99%)
    pallas_call x1, Pallas kernels, on_device(): pl.pallas_call(functools.partial(layer_kernel, dims), out_shape=(shape, s...  66.4 us
    pallas_call x1, Pallas kernels, on_device(): pl.pallas_call(write_kernel, out_shape=(shape, shape), in_specs=[any_spac...  1.97 us

profile of v6, /device:TPU:1, one launch (start us, length us, event | category | flops | bytes accessed | tf_op | source)
XLA Modules:
  0.0 69.0 jit_solution(8324390640248023914)
XLA Ops:
  0.6 66.4 %shard_map.86 = (bf16[64,3584]{1,0:T(8,128)(2,1)}, bf16[64,3584]{1,0:T(8,128)(2,1)}) custom-call(s32[1,64]{1,0:T(1,128)} %bitcast.16, s32[1,64]{1,0:T(1,128)} %bitcast.17, bf16[64,3584]{1,0:T(8,128)(2,1)} %bitcast.13, bf16[64,3584]{1,0:T(8,128)(2,1)} %bitcast.14, f32[4,3584]{1,0:T(4,128)} %bitcast.15, bf16[3584,512]{1,0:T(8,128)(2,1)} %bitcast.11, ...), custom_call_target="tpu_custom_call" | custom-call | tf_op jit(solution)/shard_map/pallas_call | solution.py:319
  67.1 2.0 %shard_map.87 = (bf16[64,3584]{1,0:T(8,128)(2,1)}, bf16[64,3584]{1,0:T(8,128)(2,1)}) custom-call(bf16[64,3584]{1,0:T(8,128)(2,1)} %get-tuple-element.6.a_ref, bf16[64,3584]{1,0:T(8,128)(2,1)} %get-tuple-element.7.b_ref), custom_call_target="tpu_custom_call" | custom-call | tf_op jit(solution)/shard_map/pallas_call | solution.py:361
